TPU v7x, 32 devices: a whole 2x2x4 slice. The times are simulated.
32 devices in a mesh: occ: 8 (over z, x), aux: 4 (over y, core).
Axes of the slice: x: 2, y: 2, z: 4, core: 2. Of those that a mesh axis runs over, the one named last changes fastest.
Arguments:
- int_tiles: bfloat16 [32, 64, 128, 256], P('occ', 'aux'), may hold values from -0.5 to 0.5
- tile_ids: int32 [32, 64], P('occ', 'aux'), may hold values from 0 to 79, as said below
- tile_counts: int32 [32, 4], P('occ', 'aux'), may hold values from 8 to 16, as said below
- pair_list: int32 [64, 2], P('occ'), may hold values from 0 to 3
- occ_energy: float32 [32], replicated, may hold values from -2 to -0.5
- vir_energy: float32 [256], replicated, may hold values from 0.2 to 3
Outputs:
- gamma_tiles: bfloat16 [32, 64, 128, 256], P('occ', 'aux')
- density: float32 [256, 256], P('aux')
Inputs may be any that keep to these rules, and one draw needn't show every extreme that they name: `tile_ids`: within one orbital and one aux index's share the 16 tile numbers are distinct. Only the first tile_counts slots of a share are live; tiles and numbers of the others are never read. `pair_list`: column 0 indexes the asking occ index's orbitals, column 1 those of occ index r.
All inputs are finite; a program needn't handle non-finite values.
Results may differ from a plain program's by a relative error of at most 0.0085.
Values may be sent and summed in bfloat16 or wider, within the bound.
A program may use at most 256 MiB of HBM per device.

v0:
```python
import jax
import jax.numpy as jnp
from jax import lax
from jax.sharding import PartitionSpec as P


def amplitudes(coulomb, energy_pair, vir_energy):
    denominator = energy_pair[:, None, None] - vir_energy[None, :, None] - vir_energy[None, None, :]
    amplitude = coulomb / denominator
    return (amplitude, 2.0 * amplitude - jnp.swapaxes(amplitude, 1, 2))


def density_terms(amplitude_left, amplitude_right, spin_mixed):
    first_term = jnp.einsum(
        "rac,rbc->ab", amplitude_left, spin_mixed, precision=lax.Precision.HIGHEST
    )
    second_term = jnp.einsum(
        "rca,rcb->ab", amplitude_right, spin_mixed, precision=lax.Precision.HIGHEST
    )
    return first_term + second_term


def per_device(int_tiles, tile_ids, tile_counts, pair_list, occ_energy, vir_energy):
    peer_count = lax.axis_size("occ")
    group_count = lax.axis_size("aux")
    orb_count = int_tiles.shape[0]
    slot_count = int_tiles.shape[1]
    tile_rows = int_tiles.shape[2]
    virt_width = int_tiles.shape[3]
    pair_count = pair_list.shape[0]
    per_peer = pair_count // peer_count
    block_shape = (peer_count, per_peer, slot_count, tile_rows, virt_width)
    my_first = lax.axis_index("occ") * orb_count
    counts = tile_counts[:, 0]
    source = jnp.arange(pair_count, dtype=jnp.int32) // per_peer
    wanted = pair_list[:, 1]
    asked_for = lax.all_to_all(
        wanted.reshape(peer_count, per_peer), "occ", split_axis=0, concat_axis=0, tiled=True
    ).reshape(pair_count)
    arrived = (
        lax.all_to_all(
            int_tiles[asked_for].reshape(block_shape),
            "occ",
            split_axis=0,
            concat_axis=0,
            tiled=True,
        ),
        lax.all_to_all(
            tile_ids[asked_for].reshape(peer_count, per_peer, slot_count),
            "occ",
            split_axis=0,
            concat_axis=0,
            tiled=True,
        ),
        lax.all_to_all(
            counts[asked_for].reshape(peer_count, per_peer),
            "occ",
            split_axis=0,
            concat_axis=0,
            tiled=True,
        ),
    )
    here_index = pair_list[:, 0]
    there_global = source * orb_count + wanted
    there_tiles, there_ids, there_counts = arrived
    there_tiles = there_tiles.reshape(pair_count, slot_count, tile_rows, virt_width)
    there_ids = there_ids.reshape(pair_count, slot_count)
    there_counts = there_counts.reshape(pair_count)
    energy_pair = occ_energy[my_first + here_index] + occ_energy[there_global]
    slot_range = jnp.arange(slot_count, dtype=jnp.int32)

    def intersection_of(pair_index):
        here_orb = here_index[pair_index]
        here_live = slot_range < counts[here_orb]
        there_live = slot_range < there_counts[pair_index]
        same_tile = tile_ids[here_orb][:, None] == there_ids[pair_index][None, :]
        intersection = (same_tile & here_live[:, None] & there_live[None, :]).astype(jnp.bfloat16)
        return (int_tiles[here_orb], intersection)

    def rows_of_there(intersection, pair_index):
        return jnp.einsum(
            "st,tpb->spb", intersection, there_tiles[pair_index], preferred_element_type=jnp.float32
        ).astype(jnp.bfloat16)

    def coulomb_term(running, pair_index):
        here_block, intersection = intersection_of(pair_index)
        rows_there = rows_of_there(intersection, pair_index)
        term = lax.dot_general(
            here_block.reshape(-1, virt_width),
            rows_there.reshape(-1, virt_width),
            (((0,), (0,)), ((), ())),
            preferred_element_type=jnp.float32,
        )
        return (running, term)

    pair_range = jnp.arange(pair_count, dtype=jnp.int32)
    unused, partial_terms = lax.scan(coulomb_term, 0, pair_range)
    coulomb = lax.psum(partial_terms, "aux")
    amplitude, spin_mixed = amplitudes(coulomb, energy_pair, vir_energy)
    row_block = virt_width // group_count
    row_start = lax.axis_index("aux") * row_block
    amplitude_rows = lax.dynamic_slice_in_dim(amplitude, row_start, row_block, 1)
    amplitude_cols = lax.dynamic_slice_in_dim(amplitude, row_start, row_block, 2)
    density = density_terms(amplitude_rows, amplitude_cols, spin_mixed)
    weights = spin_mixed.astype(jnp.bfloat16)
    density = lax.psum(density.astype(jnp.bfloat16), "occ").astype(jnp.float32)
    part_shape = (slot_count, tile_rows, virt_width)

    def gamma_term(running, pair_index):
        here_block, intersection = intersection_of(pair_index)
        rows_there = rows_of_there(intersection, pair_index)
        rows_here = jnp.einsum(
            "st,spa->tpa", intersection, here_block, preferred_element_type=jnp.float32
        ).astype(jnp.bfloat16)
        pair_weights = weights[pair_index]
        here_part = lax.dot_general(
            rows_there.reshape(-1, virt_width),
            pair_weights,
            (((1,), (1,)), ((), ())),
            preferred_element_type=jnp.float32,
        )
        there_part = jnp.dot(
            rows_here.reshape(-1, virt_width), pair_weights, preferred_element_type=jnp.float32
        )
        return (
            running,
            (
                here_part.astype(jnp.bfloat16).reshape(part_shape),
                there_part.astype(jnp.bfloat16).reshape(part_shape),
            ),
        )

    unused, parts = lax.scan(gamma_term, 0, pair_range)
    here_parts, there_parts = parts
    returned = lax.all_to_all(
        there_parts.reshape(block_shape), "occ", split_axis=0, concat_axis=0, tiled=True
    ).reshape(pair_count, slot_count, tile_rows, virt_width)
    gamma_sum = jnp.zeros((orb_count, slot_count, tile_rows, virt_width), jnp.float32)
    gamma_sum = gamma_sum.at[here_index].add(here_parts.astype(jnp.float32))
    gamma_sum = gamma_sum.at[asked_for].add(returned.astype(jnp.float32))
    return (gamma_sum.astype(jnp.bfloat16), density)


def solution(mesh):
    placed = (
        P("occ", "aux", None, None),
        P("occ", "aux"),
        P("occ", "aux"),
        P("occ", None),
        P(),
        P(),
    )
    return jax.shard_map(
        per_device,
        mesh=mesh,
        in_specs=placed,
        out_specs=(P("occ", "aux", None, None), P("aux", None)),
        check_vma=False,
    )
```

profile of v0, /device:TPU:0, one launch (start us, length us, event | category | flops | bytes accessed | tf_op | source)
XLA Modules:
  0.0 811.5 jit_solution(979739568386542824)
XLA Ops:
  8.0 13.5 %all_to_all.36 = s32[8,1,1]{2,1,0:T(1,128)S(1)} all-to-all(s32[8,1,1]{2,1,0:T(1,128)S(1)} %copy.47), channel_id=1, replica_groups=mesh['occ'=8,'aux'=4] {'occ'}, dimensions={0} | all-to-all | bytes 64 | tf_op jit(solution)/shard_map/all_to_all | solution.py:37
  21.8 1.3 gather_fusion.1
  23.8 3.3 all-to-all-start.2
  27.1 6.9 gather_fusion.2
  34.0 6.0 all-to-all-start.3
  41.1 180.3 %all-to-all-done.3 = bf16[8,1,16,128,256]{4,3,2,1,0:T(8,128)(2,1)} async-done(((bf16[8,1,16,128,256]{4,3,2,1,0:T(8,128)(2,1)}), bf16[8,1,16,128,256]{4,3,2,1,0:T(8,128)(2,1)}, u32[]{:S(2)}, u32[]{:S(2)}) %all-to-all-start.3) | async-done | bytes 8388640 | tf_op jit(solution)/shard_map/all_to_all | solution.py:41
  221.4 3.6 all-to-all-start.1
  225.4 11.8 %copy.53 = bf16[8,16,128,256]{3,1,2,0:T(8,128)(2,1)} copy(bf16[8,16,128,256]{3,2,1,0:T(8,128)(2,1)} %bitcast.11) | data formatting | bytes 16777216
  237.2 96.8 %while.26 = (s32[]{:T(128)}, f32[8,256,256]{2,1,0:T(8,128)}, s32[8]{0:T(128)S(1)}, s32[8]{0:T(128)S(1)}, bf16[4,16,128,256]{3,2,1,0:T(8,128)(2,1)}, /*index=5*/s...) while((s32[]{:T(128)}, f32[8,256,256]{2,1,0:T(8,128)}, ...), condition=%wide.region_1.2_spmd.clone.clone, body=%wide.region_0.1_spmd.clone.clone.sunk | while | flops 285737760 | bytes 8651985 | solution.py:97
  244.8 1.7 convolution_convert_fusion.10
  246.8 1.3 constant_dynamic-slice_fusion.8
  256.9 1.7 convolution_convert_fusion.10
  258.9 1.3 constant_dynamic-slice_fusion.8
  269.0 1.7 convolution_convert_fusion.10
  271.0 1.3 constant_dynamic-slice_fusion.8
  281.1 1.7 convolution_convert_fusion.10
  283.1 1.3 constant_dynamic-slice_fusion.8
  293.2 1.7 convolution_convert_fusion.10
  295.2 1.3 constant_dynamic-slice_fusion.8
  305.3 1.7 convolution_convert_fusion.10
  307.3 1.3 constant_dynamic-slice_fusion.8
  317.4 1.7 convolution_convert_fusion.10
  319.4 1.3 constant_dynamic-slice_fusion.8
  329.5 1.7 convolution_convert_fusion.10
  331.5 1.3 constant_dynamic-slice_fusion.8
  335.5 51.5 %all-reduce.2.cloned.1.call-done = f32[8,256,256]{2,1,0:T(8,128)} async-done(((f32[8,256,256]{2,1,0:T(8,128)}), f32[8,256,256]{2,1,0:T(8,128)}) %all-reduce.2.cloned.1.call-update) | async-done | bytes 2097168 | tf_op jit(solution)/shard_map/psum | solution.py:98
  387.0 1.9 subtract_divide_fusion
  388.9 1.8 copy.52
  390.7 2.7 fusion.49
  393.4 115.8 %while.27 = (s32[]{:T(128)}, bf16[8,16,128,256]{3,2,1,0:T(8,128)(2,1)}, bf16[8,16,128,256]{3,2,1,0:T(8,128)(2,1)}, s32[8]{0:T(128)S(1)}, s32[8]{0:T(128)S(1)}, /...) while((s32[]{:T(128)}, ...), condition=%wide.region_4.5_spmd.clone.clone, body=%wide.region_3.4_spmd.clone.clone.sunk | while | flops 572524032 | bytes 19137928 | solution.py:133
  398.4 1.3 constant_dynamic-slice_fusion.9
  403.8 1.8 convolution_convert_fusion.13
  406.4 1.5 constant_dynamic-update-slice_fusion.3
  413.0 1.3 constant_dynamic-slice_fusion.9
  418.4 1.8 convolution_convert_fusion.13
  420.9 1.5 constant_dynamic-update-slice_fusion.3
  427.5 1.3 constant_dynamic-slice_fusion.9
  432.9 1.8 convolution_convert_fusion.13
  435.4 1.5 constant_dynamic-update-slice_fusion.3
  441.9 1.3 constant_dynamic-slice_fusion.9
  447.3 1.8 convolution_convert_fusion.13
  449.9 1.5 constant_dynamic-update-slice_fusion.3
  456.4 1.3 constant_dynamic-slice_fusion.9
  461.8 1.8 convolution_convert_fusion.13
  464.3 1.5 constant_dynamic-update-slice_fusion.3
  470.9 1.3 constant_dynamic-slice_fusion.9
  476.3 1.8 convolution_convert_fusion.13
  478.8 1.4 constant_dynamic-update-slice_fusion.3
  485.3 1.3 constant_dynamic-slice_fusion.9
  490.7 1.8 convolution_convert_fusion.13
  493.3 1.5 constant_dynamic-update-slice_fusion.3
  499.8 1.3 constant_dynamic-slice_fusion.9
  505.2 1.8 convolution_convert_fusion.13
  507.8 1.4 constant_dynamic-update-slice_fusion.3
  509.2 5.5 all-to-all-start.4
  514.8 11.6 %convert_element_type.39 = f32[8,16,128,256]{3,2,1,0:T(8,128)} convert(bf16[8,16,128,256]{3,2,1,0:T(8,128)(2,1)} %get-tuple-element.134) | non-fusion elementwise | flops 4194304 | bytes 25165824 | tf_op jit(solution)/shard_map/convert_element_type | solution.py:139
  526.4 1.3 convolution_bitcast_fusion.2
  527.7 2.5 fusion.40
  530.2 190.8 %psum.15 = bf16[64,256]{1,0:T(8,128)(2,1)S(1)} all-reduce(bf16[64,256]{1,0:T(8,128)(2,1)S(1)} %fusion.40), channel_id=1, replica_groups=mesh['occ'=8,'aux'=4] {'occ'}, use_global_device_ids=true, to_apply=%region_7.8 | all-reduce | flops 16384 | bytes 65536 | tf_op jit(solution)/shard_map/psum | solution.py:106
  721.6 4.3 broadcast_in_dim.16
  725.9 30.6 %scatter_fusion = f32[4,16,128,256]{3,2,1,0:T(8,128)} fusion(f32[4,16,128,256]{3,2,1,0:T(8,128)} %broadcast_in_dim.16, s32[8]{0:T(128)S(1)} %get-tuple-element.370, f32[8,16,128,256]{3,2,1,0:T(8,128)} %convert_element_type.39), kind=kCustom, calls=%fused_computation.5 | custom fusion | flops 4194304 | bytes 50331680 | tf_op jit(solution)/shard_map/scatter-add | solution.py:139
  756.5 11.5 %bitcast_convert_fusion = f32[8,16,128,256]{3,2,1,0:T(8,128)} fusion(bf16[8,1,16,128,256]{4,3,2,1,0:T(8,128)(2,1)} %all-to-all-done.4), kind=kLoop, calls=%fused_computation.64 | loop fusion | flops 4194304 | bytes 25165824 | tf_op jit(solution)/shard_map/convert_element_type | solution.py:140
  768.0 30.6 %scatter_fusion.1 = f32[4,16,128,256]{3,2,1,0:T(8,128)} fusion(f32[4,16,128,256]{3,2,1,0:T(8,128)} %scatter_fusion, s32[8]{0:T(128)S(1)} %fusion.44, f32[8,16,128,256]{3,2,1,0:T(8,128)} %bitcast_convert_fusion), kind=kCustom, calls=%fused_computation.6 | custom fusion | flops 4194304 | bytes 50331680 | tf_op jit(solution)/shard_map/scatter-add | solution.py:140
  798.6 6.0 convert_element_type.42
  (204 shorter events, 94.9 us)
Async XLA Ops:
  7.2 326.9 %copy-start = (f32[32]{0:T(128)S(1)}, f32[32]{0:T(128)}, u32[]{:S(2)}) copy-start(f32[32]{0:T(128)} %param.14) | copy-start | bytes 388
  23.8 10.2 %all-to-all-start.2 = ((s32[8,1,1]{2,1,0:T(1,128)}), s32[8,1,1]{2,1,0:T(1,128)S(1)}, u32[]{:S(2)}, u32[]{:S(2)}) async-start(s32[8,1,1]{2,1,0:T(1,128)} %copy.49), calls=%async_computation.2 | async-start | bytes 8192 | tf_op jit(solution)/shard_map/all_to_all | solution.py:55
  34.0 6.0 copy-start.4
  34.0 187.5 %all-to-all-start.3 = ((bf16[8,1,16,128,256]{4,3,2,1,0:T(8,128)(2,1)}), bf16[8,1,16,128,256]{4,3,2,1,0:T(8,128)(2,1)}, u32[]{:S(2)}, u32[]{:S(2)}) async-start(bf16[8,1,16,128,256]{4,3,2,1,0:T(8,128)(2,1)} %bitcast.165), calls=%async_computation.3 | async-start | bytes 16777216 | tf_op jit(solution)/shard_map/all_to_all | solution.py:41
  221.4 15.7 %all-to-all-start.1 = ((s32[8,1,16]{2,1,0:T(1,128)}), s32[8,1,16]{2,1,0:T(1,128)S(1)}, u32[]{:S(2)}, u32[]{:S(2)}) async-start(s32[8,1,16]{2,1,0:T(1,128)} %bitcast.5), calls=%async_computation.1 | async-start | bytes 8192 | tf_op jit(solution)/shard_map/all_to_all | solution.py:48
  225.1 161.9 %all-reduce.2.cloned.1.call-start = ((), (), s32[]{:S(2)}) async-start(), calls=%async_computation.5 | async-start | bytes 4194304 | tf_op jit(solution)/shard_map/psum | solution.py:98
  225.3 11.8 %copy-start.2 = (s32[4,1]{0,1:T(1,128)S(1)}, s32[4,1]{0,1:T(1,128)}, u32[]{:S(2)}) copy-start(s32[4,1]{0,1:T(1,128)} %param.12) | copy-start | bytes 52
  237.2 98.2 %copy-start.5 = (f32[256]{0:T(256)S(1)}, f32[256]{0:T(256)}, u32[]{:S(2)}) copy-start(f32[256]{0:T(256)} %param.15) | copy-start | bytes 3076
  509.2 247.3 %all-to-all-start.4 = ((bf16[8,1,16,128,256]{4,3,2,1,0:T(8,128)(2,1)}), bf16[8,1,16,128,256]{4,3,2,1,0:T(8,128)(2,1)}, u32[]{:S(2)}, u32[]{:S(2)}) async-start(bf16[8,1,16,128,256]{4,3,2,1,0:T(8,128)(2,1)} %bitcast.166), calls=%async_computation.4 | async-start | bytes 16777216 | tf_op jit(solution)/shard_map/all_to_all | solution.py:135
  514.8 11.6 %copy-start.3 = (f32[8,256,256]{1,2,0:T(8,128)S(1)}, f32[8,256,256]{1,2,0:T(8,128)}, u32[]{:S(2)}) copy-start(f32[8,256,256]{1,2,0:T(8,128)} %copy.52) | copy-start | bytes 6291460
  768.0 36.6 %copy-start.1 = (f32[32]{0:T(128)S(1)}, f32[32]{0:T(128)}, u32[]{:S(2)}) copy-start(f32[32]{0:T(128)} %param.14) | copy-start | bytes 388
Sparse Core Ops, SparseCore 0:
  334.2 52.7 all-reduce.1
where the time goes:
time: 815 us; the launch traced here: 811 us
  waiting for transfers between devices  232 us (28%)
  blocking collectives  204 us (25%)
  other arithmetic  117 us (14%)
  local copies, waits for them, and re-layouts  109 us (13%)
  loops' own time  62.4 us (8%)
  matrix products  54.3 us (7%)
  starting transfers between devices  18.5 us (2%)
  between operations  14.2 us (2%)
    psum x1, blocking collectives, per_device(): density = lax.psum(density.astype(jnp.bfloat16), 'occ').astype(jnp.float32)  191 us
    all_to_all x1, waiting for transfers between devices, per_device(): lax.all_to_all(int_tiles[asked_for].reshape(block_shape), 'occ', split_ax...  180 us
    psum x1, waiting for transfers between devices, per_device(): coulomb = lax.psum(partial_terms, 'aux')  51.5 us
    another operation x1, loops' own time, per_device(): unused, partial_terms = lax.scan(coulomb_term, 0, pair_range)  31.4 us
    another operation x1, loops' own time, per_device(): unused, parts = lax.scan(gamma_term, 0, pair_range)  31 us
    scatter-add x1, other arithmetic, per_device(): gamma_sum = gamma_sum.at[here_index].add(here_parts.astype(jnp.float32))  30.6 us
    scatter-add x1, other arithmetic, per_device(): gamma_sum = gamma_sum.at[asked_for].add(returned.astype(jnp.float32))  30.6 us
    dot_general x16, matrix products, rows_of_there(): jnp.einsum('st,tpb->spb', intersection, there_tiles[pair_index], preferre...  27.9 us
  transfers between devices with their start and end apart: 5, of which 2 were waited for; matrix products, arithmetic and copies ran while one was open for 9% of the time, Pallas kernels for 0%

commit v1 on v0

--- a/solution.py
+++ b/solution.py
@@ -1,7 +1,45 @@
+import functools
 import jax
 import jax.numpy as jnp
 from jax import lax
 from jax.sharding import PartitionSpec as P
+
+
+def settle_sheet(patch, axis_no, mine):
+    piece_out = patch.shape
+    return jnp.moveaxis(
+        patch.reshape(
+            *piece_out[:axis_no], mine, piece_out[axis_no] // mine, *piece_out[axis_no + 1 :]
+        ),
+        axis_no,
+        0,
+    )
+
+
+def set_the_widths(base_x, in_dim):
+    r1 = list(base_x.shape[1:])
+    r1[in_dim] *= base_x.shape[0]
+    return jnp.moveaxis(base_x, 0, in_dim).reshape(r1)
+
+
+def end_the_array(shard_in, across, mine_x, my_tile):
+    piece_now = lax.psum(1, across)
+    answer = lax.axis_index(across)
+    current_block, small = (piece_now, answer)
+    u1 = settle_sheet(shard_in, mine_x, current_block)
+    shelf = [u1[small]]
+    for no in range(1, current_block):
+        part_next = u1[small ^ no]
+        kept_arr = lax.ppermute(
+            part_next, across, [(src_i, src_i ^ no) for src_i in range(current_block)]
+        )
+        shelf.append(kept_arr)
+    passed = jnp.stack(shelf, 0)
+    u1 = passed[small ^ jnp.arange(current_block)]
+    return set_the_widths(u1, my_tile)
+
+
+plan_the_tasks = functools.partial(end_the_array, across="occ", mine_x=0, my_tile=0)
 
 
 def amplitudes(coulomb, energy_pair, vir_energy):
@@ -38,13 +76,7 @@
         wanted.reshape(peer_count, per_peer), "occ", split_axis=0, concat_axis=0, tiled=True
     ).reshape(pair_count)
     arrived = (
-        lax.all_to_all(
-            int_tiles[asked_for].reshape(block_shape),
-            "occ",
-            split_axis=0,
-            concat_axis=0,
-            tiled=True,
-        ),
+        plan_the_tasks(int_tiles[asked_for].reshape(block_shape)),
         lax.all_to_all(
             tile_ids[asked_for].reshape(peer_count, per_peer, slot_count),
             "occ",

time: 815 us -> 830 us (1.018)
  local copies, waits for them, and re-layouts: 109 us -> 140 us
  waiting for transfers between devices: 232 us -> 207 us
  starting transfers between devices: 18.5 us -> 30.9 us
    all_to_all x1, waiting for transfers between devices: 180 us -> 6.39 us  [per_device(): lax.all_to_all(wanted.reshape(peer_count, per_peer), 'occ', split_axis=0,...]
    all_to_all x1, waiting for transfers between devices: 0.01 us -> 80.3 us  [per_device(): lax.all_to_all(counts[asked_for].reshape(peer_count, per_peer), 'occ', sp...]
    psum x1, waiting for transfers between devices: 51.5 us -> 92.3 us  [per_device(): coulomb = lax.psum(partial_terms, 'aux')]
    ppermute x0 -> x7, waiting for transfers between devices: none -> 27.5 us  [end_the_array(): lax.ppermute(part_next, across, [(src_i, src_i ^ no) for src_i in range(c...]
    unnamed x13 -> x18, local copies, waits for them, and re-layouts: 11.8 us -> 26.8 us
    all_to_all x1 -> x0, blocking collectives: 13.5 us -> none  [per_device(): lax.all_to_all(wanted.reshape(peer_count, per_peer), 'occ', split_axis=0,...]
    ppermute x0 -> x7, starting transfers between devices: none -> 11.5 us  [end_the_array(): lax.ppermute(part_next, across, [(src_i, src_i ^ no) for src_i in range(c...]
    psum x1, blocking collectives: 191 us -> 199 us  [per_device(): density = lax.psum(density.astype(jnp.bfloat16), 'occ').astype(jnp.float32)]
  transfers between devices with their start and end apart: 5 -> 12, of which waited for: 2 -> 5; matrix products, arithmetic and copies ran while one was open for 9% -> 11% of each run, Pallas kernels for 0% -> 0%
where the time goes in v1:
time: 830 us; the launch traced here: 827 us
  waiting for transfers between devices  207 us (25%)
  blocking collectives  199 us (24%)
  local copies, waits for them, and re-layouts  140 us (17%)
  other arithmetic  117 us (14%)
  loops' own time  61.8 us (7%)
  matrix products  57.5 us (7%)
  starting transfers between devices  30.9 us (4%)
  between operations  14.2 us (2%)
    psum x1, blocking collectives, per_device(): density = lax.psum(density.astype(jnp.bfloat16), 'occ').astype(jnp.float32)  199 us
    psum x1, waiting for transfers between devices, per_device(): coulomb = lax.psum(partial_terms, 'aux')  92.3 us
    all_to_all x1, waiting for transfers between devices, per_device(): lax.all_to_all(counts[asked_for].reshape(peer_count, per_peer), 'occ', sp...  80.3 us
    another operation x1, loops' own time, per_device(): unused, partial_terms = lax.scan(coulomb_term, 0, pair_range)  31.4 us
    scatter-add x1, other arithmetic, per_device(): gamma_sum = gamma_sum.at[here_index].add(here_parts.astype(jnp.float32))  30.6 us
    scatter-add x1, other arithmetic, per_device(): gamma_sum = gamma_sum.at[asked_for].add(returned.astype(jnp.float32))  30.6 us
    another operation x1, loops' own time, per_device(): unused, parts = lax.scan(gamma_term, 0, pair_range)  30.4 us
    dot_general x16, matrix products, rows_of_there(): jnp.einsum('st,tpb->spb', intersection, there_tiles[pair_index], preferre...  27.9 us
  transfers between devices with their start and end apart: 12, of which 5 were waited for; matrix products, arithmetic and copies ran while one was open for 11% of the time, Pallas kernels for 0%

profile of v1, /device:TPU:0, one launch (start us, length us, event | category | flops | bytes accessed | tf_op | source)
XLA Modules:
  0.0 827.0 jit_solution(12980642913439680115)
XLA Ops:
  8.6 7.3 all-to-all-start
  15.9 6.4 all-to-all-done
  22.5 6.9 gather_fusion.2
  29.4 5.6 dynamic-slice_bitcast_fusion
  36.1 2.4 collective-permute-start.2
  39.0 2.3 collective-permute-start.4
  42.6 3.3 all-to-all-start.2
  45.9 2.4 bitcast_dynamic-update-slice_fusion.7
  49.5 80.3 %all-to-all-done.2 = s32[8,1,1]{2,1,0:T(1,128)S(1)} async-done(((s32[8,1,1]{2,1,0:T(1,128)}), s32[8,1,1]{2,1,0:T(1,128)S(1)}, u32[]{:S(2)}, u32[]{:S(2)}) %all-to-all-start.2) | async-done | bytes 64 | tf_op jit(solution)/shard_map/all_to_all | solution.py:87
  129.8 3.3 all-to-all-start.1
  133.4 3.8 collective-permute-start.5
  137.1 2.3 bitcast_dynamic-update-slice_fusion.6
  139.4 1.4 collective-permute-start.6
  140.8 2.3 bitcast_dynamic-update-slice_fusion.5
  143.2 2.3 bitcast_dynamic-update-slice_fusion.4
  145.5 2.4 bitcast_dynamic-update-slice_fusion.3
  147.9 2.3 bitcast_dynamic-update-slice_fusion.2
  150.2 11.2 %collective-permute-done.5 = bf16[1,1,16,128,256]{4,3,2,1,0:T(8,128)(2,1)S(1)} collective-permute-done((bf16[1,1,16,128,256]{4,3,2,1,0:T(8,128)(2,1)S(1)}, bf16[1,1,16,128,256]{4,3,2,1,0:T(8,128)(2,1)S(1)}, u32[]{:S(2)}, u32[]{:S(2)}) %collective-permute-start.5) | collective-permute-done | bytes 1048608 | tf_op jit(solution)/shard_map/ppermute | solution.py:33
  162.4 16.3 %collective-permute-done.6 = bf16[1,1,16,128,256]{4,3,2,1,0:T(8,128)(2,1)S(1)} collective-permute-done((bf16[1,1,16,128,256]{4,3,2,1,0:T(8,128)(2,1)S(1)}, bf16[1,1,16,128,256]{4,3,2,1,0:T(8,128)(2,1)S(1)}, u32[]{:S(2)}, u32[]{:S(2)}) %collective-permute-start.6) | collective-permute-done | bytes 1048608 | tf_op jit(solution)/shard_map/ppermute | solution.py:33
  179.8 8.2 gather_fusion.3
  188.0 11.8 %copy.51 = bf16[8,16,128,256]{3,1,2,0:T(8,128)(2,1)} copy(bf16[8,16,128,256]{3,2,1,0:T(8,128)(2,1)} %gather_fusion.3) | data formatting | bytes 16777216
  199.8 97.0 %while.26 = (s32[]{:T(128)}, f32[8,256,256]{2,1,0:T(8,128)}, s32[8]{0:T(128)S(1)}, s32[8]{0:T(128)S(1)}, bf16[4,16,128,256]{3,2,1,0:T(8,128)(2,1)}, /*index=5*/s...) while((s32[]{:T(128)}, f32[8,256,256]{2,1,0:T(8,128)}, ...), condition=%wide.region_1.2_spmd.clone.clone, body=%wide.region_0.1_spmd.clone.clone.sunk | while | flops 285737760 | bytes 8651985 | solution.py:129
  207.4 1.7 convolution_convert_fusion.10
  219.6 1.7 convolution_convert_fusion.10
  231.7 1.7 convolution_convert_fusion.10
  233.7 1.3 constant_dynamic-slice_fusion.8
  243.8 1.7 convolution_convert_fusion.10
  245.9 1.3 constant_dynamic-slice_fusion.8
  255.9 1.7 convolution_convert_fusion.10
  268.1 1.7 convolution_convert_fusion.10
  280.2 1.7 convolution_convert_fusion.10
  292.3 1.7 convolution_convert_fusion.10
  294.4 1.3 constant_dynamic-slice_fusion.8
  298.3 92.3 %all-reduce.2.cloned.1.call-done = f32[8,256,256]{2,1,0:T(8,128)} async-done(((f32[8,256,256]{2,1,0:T(8,128)}), f32[8,256,256]{2,1,0:T(8,128)}) %all-reduce.2.cloned.1.call-update) | async-done | bytes 2097168 | tf_op jit(solution)/shard_map/psum | solution.py:130
  390.6 1.9 subtract_divide_fusion
  392.5 1.8 copy.50
  394.4 2.7 fusion.50
  397.0 116.3 %while.27 = (s32[]{:T(128)}, bf16[8,16,128,256]{3,2,1,0:T(8,128)(2,1)}, bf16[8,16,128,256]{3,2,1,0:T(8,128)(2,1)}, s32[8]{0:T(128)S(1)}, s32[8]{0:T(128)S(1)}, /...) while((s32[]{:T(128)}, ...), condition=%wide.region_4.5_spmd.clone.clone, body=%wide.region_3.4_spmd.clone.clone.sunk | while | flops 572524032 | bytes 19137928 | solution.py:165
  407.5 1.8 convolution_convert_fusion.13
  410.1 1.5 constant_dynamic-update-slice_fusion.3
  422.1 1.8 convolution_convert_fusion.13
  424.7 1.5 constant_dynamic-update-slice_fusion.3
  436.7 1.8 convolution_convert_fusion.13
  439.2 1.5 constant_dynamic-update-slice_fusion.3
  451.2 1.8 convolution_convert_fusion.13
  453.7 1.5 constant_dynamic-update-slice_fusion.3
  465.7 1.8 convolution_convert_fusion.13
  468.3 1.5 constant_dynamic-update-slice_fusion.3
  480.3 1.8 convolution_convert_fusion.13
  482.8 1.5 constant_dynamic-update-slice_fusion.3
  494.8 1.8 convolution_convert_fusion.13
  497.4 1.5 constant_dynamic-update-slice_fusion.3
  509.3 1.8 convolution_convert_fusion.13
  511.9 1.4 constant_dynamic-update-slice_fusion.3
  513.3 5.5 all-to-all-start.3
  518.8 2.9 convolution_bitcast_fusion.2
  521.7 4.1 fusion.40
  525.8 199.3 %psum.15 = bf16[64,256]{1,0:T(8,128)(2,1)S(1)} all-reduce(bf16[64,256]{1,0:T(8,128)(2,1)S(1)} %fusion.40), channel_id=1, replica_groups=mesh['occ'=8,'aux'=4] {'occ'}, use_global_device_ids=true, to_apply=%region_7.8 | all-reduce | flops 16384 | bytes 65536 | tf_op jit(solution)/shard_map/psum | solution.py:138
  725.7 11.5 %convert_element_type.39 = f32[8,16,128,256]{3,2,1,0:T(8,128)} convert(bf16[8,16,128,256]{3,2,1,0:T(8,128)(2,1)} %get-tuple-element.134) | non-fusion elementwise | flops 4194304 | bytes 25165824 | tf_op jit(solution)/shard_map/convert_element_type | solution.py:171
  737.2 4.3 broadcast_in_dim.16
  741.5 30.6 %scatter_fusion = f32[4,16,128,256]{3,2,1,0:T(8,128)} fusion(f32[4,16,128,256]{3,2,1,0:T(8,128)} %broadcast_in_dim.16, s32[8]{0:T(128)S(1)} %get-tuple-element.377, f32[8,16,128,256]{3,2,1,0:T(8,128)} %convert_element_type.39), kind=kCustom, calls=%fused_computation.6 | custom fusion | flops 4194304 | bytes 50331680 | tf_op jit(solution)/shard_map/scatter-add | solution.py:171
  772.1 11.5 %bitcast_convert_fusion = f32[8,16,128,256]{3,2,1,0:T(8,128)} fusion(bf16[8,1,16,128,256]{4,3,2,1,0:T(8,128)(2,1)} %all-to-all-done.3), kind=kLoop, calls=%fused_computation.65 | loop fusion | flops 4194304 | bytes 25165824 | tf_op jit(solution)/shard_map/convert_element_type | solution.py:172
  783.6 30.6 %scatter_fusion.1 = f32[4,16,128,256]{3,2,1,0:T(8,128)} fusion(f32[4,16,128,256]{3,2,1,0:T(8,128)} %scatter_fusion, s32[8]{0:T(128)S(1)} %fusion.46, f32[8,16,128,256]{3,2,1,0:T(8,128)} %bitcast_convert_fusion), kind=kCustom, calls=%fused_computation.7 | custom fusion | flops 4194304 | bytes 50331680 | tf_op jit(solution)/shard_map/scatter-add | solution.py:172
  814.1 6.0 convert_element_type.42
  (227 shorter events, 118.1 us)
Async XLA Ops:
  7.2 289.8 %copy-start = (f32[32]{0:T(128)S(1)}, f32[32]{0:T(128)}, u32[]{:S(2)}) copy-start(f32[32]{0:T(128)} %param.14) | copy-start | bytes 388
  8.6 13.6 %all-to-all-start = ((s32[8,1,1]{2,1,0:T(1,128)}), s32[8,1,1]{2,1,0:T(1,128)S(1)}, u32[]{:S(2)}, u32[]{:S(2)}) async-start(s32[8,1,1]{2,1,0:T(1,128)} %copy.46), calls=%async_computation | async-start | bytes 8192 | tf_op jit(solution)/shard_map/all_to_all | solution.py:75
  29.4 11.9 %copy-start.2 = (s32[4,1]{0,1:T(1,128)S(1)}, s32[4,1]{0,1:T(1,128)}, u32[]{:S(2)}) copy-start(s32[4,1]{0,1:T(1,128)} %param.12) | copy-start | bytes 52
  29.4 18.9 %copy-start.3 = (s32[4,16]{1,0:T(4,128)S(1)}, s32[4,16]{1,0:T(4,128)}, u32[]{:S(2)}) copy-start(s32[4,16]{1,0:T(4,128)} %param.11) | copy-start | bytes 772
  35.0 98.4 %collective-permute-start = (bf16[1,1,16,128,256]{4,3,2,1,0:T(8,128)(2,1)}, bf16[1,1,16,128,256]{4,3,2,1,0:T(8,128)(2,1)}, u32[]{:S(2)}, u32[]{:S(2)}) collective-permute-start(bf16[1,1,16,128,256]{4,3,2,1,0:T(8,128)(2,1)} %get-tuple-element.374), channel_id=1, source_target_pairs={{0,4},{4,0},{8,12},{12,8},{16,20},{20,16},{24,28},{28,24},{1,5},{5... | collective-permute-start | bytes 3145736 | tf_op jit(solution)/shard_map/ppermute | solution.py:33
  35.4 104.0 %collective-permute-start.1 = (bf16[1,1,16,128,256]{4,3,2,1,0:T(8,128)(2,1)}, bf16[1,1,16,128,256]{4,3,2,1,0:T(8,128)(2,1)}, u32[]{:S(2)}, u32[]{:S(2)}) collective-permute-start(bf16[1,1,16,128,256]{4,3,2,1,0:T(8,128)(2,1)} %get-tuple-element.373), channel_id=1, source_target_pairs={{0,8},{4,12},{8,0},{12,4},{16,24},{20,28},{24,16},{28,20},{1,9},{5... | collective-permute-start | bytes 3145736 | tf_op jit(solution)/shard_map/ppermute | solution.py:33
  36.1 107.1 %collective-permute-start.2 = (bf16[1,1,16,128,256]{4,3,2,1,0:T(8,128)(2,1)}, bf16[1,1,16,128,256]{4,3,2,1,0:T(8,128)(2,1)}, u32[]{:S(2)}, u32[]{:S(2)}) collective-permute-start(bf16[1,1,16,128,256]{4,3,2,1,0:T(8,128)(2,1)} %get-tuple-element.372), channel_id=1, source_target_pairs={{0,12},{4,8},{8,4},{12,0},{16,28},{20,24},{24,20},{28,16},{1,13},{... | collective-permute-start | bytes 3145736 | tf_op jit(solution)/shard_map/ppermute | solution.py:33
  38.5 107.0 %collective-permute-start.3 = (bf16[1,1,16,128,256]{4,3,2,1,0:T(8,128)(2,1)}, bf16[1,1,16,128,256]{4,3,2,1,0:T(8,128)(2,1)}, u32[]{:S(2)}, u32[]{:S(2)}) collective-permute-start(bf16[1,1,16,128,256]{4,3,2,1,0:T(8,128)(2,1)} %get-tuple-element.371), channel_id=1, source_target_pairs={{0,16},{4,20},{8,24},{12,28},{16,0},{20,4},{24,8},{28,12},{1,17},{... | collective-permute-start | bytes 3145736 | tf_op jit(solution)/shard_map/ppermute | solution.py:33
  39.0 108.8 %collective-permute-start.4 = (bf16[1,1,16,128,256]{4,3,2,1,0:T(8,128)(2,1)S(1)}, bf16[1,1,16,128,256]{4,3,2,1,0:T(8,128)(2,1)}, u32[]{:S(2)}, u32[]{:S(2)}) collective-permute-start(bf16[1,1,16,128,256]{4,3,2,1,0:T(8,128)(2,1)S(1)} %get-tuple-element.370), channel_id=1, source_target_pairs={{0,20},{4,16},{8,28},{12,24},{16,4},{20,0},{24,12},{28,8},{1,21},{... | collective-permute-start | bytes 3145736 | tf_op jit(solution)/shard_map/ppermute | solution.py:33
  42.6 87.1 %all-to-all-start.2 = ((s32[8,1,1]{2,1,0:T(1,128)}), s32[8,1,1]{2,1,0:T(1,128)S(1)}, u32[]{:S(2)}, u32[]{:S(2)}) async-start(s32[8,1,1]{2,1,0:T(1,128)} %copy.48), calls=%async_computation.2 | async-start | bytes 8192 | tf_op jit(solution)/shard_map/all_to_all | solution.py:87
  129.8 70.1 %all-to-all-start.1 = ((s32[8,1,16]{2,1,0:T(1,128)}), s32[8,1,16]{2,1,0:T(1,128)S(1)}, u32[]{:S(2)}, u32[]{:S(2)}) async-start(s32[8,1,16]{2,1,0:T(1,128)} %bitcast.5), calls=%async_computation.1 | async-start | bytes 8192 | tf_op jit(solution)/shard_map/all_to_all | solution.py:80
  133.1 257.5 %all-reduce.2.cloned.1.call-start = ((), (), s32[]{:S(2)}) async-start(), calls=%async_computation.4 | async-start | bytes 4194304 | tf_op jit(solution)/shard_map/psum | solution.py:130
  133.4 28.0 %collective-permute-start.5 = (bf16[1,1,16,128,256]{4,3,2,1,0:T(8,128)(2,1)S(1)}, bf16[1,1,16,128,256]{4,3,2,1,0:T(8,128)(2,1)S(1)}, u32[]{:S(2)}, u32[]{:S(2)}) collective-permute-start(bf16[1,1,16,128,256]{4,3,2,1,0:T(8,128)(2,1)S(1)} %get-tuple-element.369), channel_id=1, source_target_pairs={{0,24},{4,28},{8,16},{12,20},{16,8},{20,12},{24,0},{28,4},{1,25},{... | collective-permute-start | bytes 3145736 | tf_op jit(solution)/shard_map/ppermute | solution.py:33
  139.4 39.3 %collective-permute-start.6 = (bf16[1,1,16,128,256]{4,3,2,1,0:T(8,128)(2,1)S(1)}, bf16[1,1,16,128,256]{4,3,2,1,0:T(8,128)(2,1)S(1)}, u32[]{:S(2)}, u32[]{:S(2)}) collective-permute-start(bf16[1,1,16,128,256]{4,3,2,1,0:T(8,128)(2,1)S(1)} %get-tuple-element.368), channel_id=1, source_target_pairs={{0,28},{4,24},{8,20},{12,16},{16,12},{20,8},{24,4},{28,0},{1,29},{... | collective-permute-start | bytes 3145736 | tf_op jit(solution)/shard_map/ppermute | solution.py:33
  199.8 98.4 %copy-start.4 = (f32[256]{0:T(256)S(1)}, f32[256]{0:T(256)}, u32[]{:S(2)}) copy-start(f32[256]{0:T(256)} %param.15) | copy-start | bytes 3076
  513.3 258.8 %all-to-all-start.3 = ((bf16[8,1,16,128,256]{4,3,2,1,0:T(8,128)(2,1)}), bf16[8,1,16,128,256]{4,3,2,1,0:T(8,128)(2,1)}, u32[]{:S(2)}, u32[]{:S(2)}) async-start(bf16[8,1,16,128,256]{4,3,2,1,0:T(8,128)(2,1)} %bitcast.195), calls=%async_computation.3 | async-start | bytes 16777216 | tf_op jit(solution)/shard_map/all_to_all | solution.py:167
  783.6 36.6 %copy-start.1 = (f32[32]{0:T(128)S(1)}, f32[32]{0:T(128)}, u32[]{:S(2)}) copy-start(f32[32]{0:T(128)} %param.14) | copy-start | bytes 388
Sparse Core Ops, SparseCore 0:
  297.0 93.5 all-reduce.1
